TPU v7x, 32 devices: a whole 2x2x4 slice. The times are simulated.
32 devices in a mesh: row: 4 (over y, core), col: 8 (over z, x).
Axes of the slice: x: 2, y: 2, z: 4, core: 2. Of those that a mesh axis runs over, the one named last changes fastest.
Arguments:
- factor: float32 [6, 2048, 6, 2048], P(None, 'row', None, 'col'), may hold values from -0.0625 to 0.0625
- diag_inv: float32 [6, 2048, 2048], P(None, None, 'row'), may hold values from -2 to 2, as said below
- structure: int32 [6, 6, 16], P(None, None, 'row'), may hold values 0 or 1
- parent: int32 [6], replicated, may hold values from 1 to 6, as said below
- post: float32 [6, 2048, 64], P(None, 'row', 'col'), may hold values from -6 to 6
Outputs:
- mean_x: float32 [6, 2048, 64], P(None, 'row', 'col')
- variance: float32 [6, 2048], P(None, 'row')
Inputs may be any that keep to these rules, and one draw needn't show every extreme that they name: parent[s] > s for s < 5, and parent[5] = 6; every supernode has at most 2 ancestors, and some supernode has exactly that many. The diagonal of each diag_inv[s] lies in 0.5 to 2.
All inputs are finite; a program needn't handle non-finite values. No bound on the sum of `structure` on one device may be relied on, other than what follows from the above.
Results may differ from a plain program's by a relative error of at most 0.00014.
Values sent between devices are 32-bit elements; how exact they have to be, the bound alone decides.
A program may use at most 192 MiB of HBM per device.

v0:
```python
import jax
import jax.numpy as jnp
from jax import lax
from jax.sharding import PartitionSpec as P

LEVELS = 3
HIGHEST = lax.Precision.HIGHEST


def contract(selected, panel_piece):
    return jnp.einsum("tiw,tin->wn", panel_piece, selected, precision=HIGHEST)


def body(factor, diag_inv, structure, parent, post):
    super_count = factor.shape[0]
    row_width = factor.shape[1]
    col_width = factor.shape[3]
    full_width = diag_inv.shape[1]
    rhs_width = post.shape[2]
    row_at = lax.axis_index("row")
    col_at = lax.axis_index("col")
    extended = jnp.concatenate([parent, jnp.full((1,), super_count, jnp.int32)])
    slot_ids = jnp.arange(super_count + 1, dtype=jnp.int32)
    targets = jnp.arange(super_count, dtype=jnp.int32)
    ancestor_hops = []
    current = parent
    for hop_index in range(super_count - 1):
        ancestor_hops.append(current)
        onehot = (current[:, None] == slot_ids[None, :]).astype(jnp.int32)
        current = jnp.sum(onehot * extended[None, :], axis=1)
    ancestry = jnp.zeros((super_count, super_count), jnp.float32)
    for hop_targets in ancestor_hops:
        ancestry = ancestry + (hop_targets[:, None] == targets[None, :]).astype(jnp.float32)
    block_rows = row_width // structure.shape[2]
    row_mask = jnp.repeat(structure.astype(jnp.float32), block_rows, axis=2) * ancestry[:, :, None]
    masked = factor * jnp.transpose(row_mask, (1, 2, 0))[:, :, :, None]
    rows_full = jnp.arange(full_width, dtype=jnp.int32)
    own_cols = row_at * row_width + jnp.arange(row_width, dtype=jnp.int32)
    lower_inv = jnp.where((rows_full[:, None] >= own_cols[None, :])[None, :, :], diag_inv, 0.0)
    unit_cols = col_at * col_width + jnp.arange(col_width, dtype=jnp.int32)
    unit_block = (rows_full[:, None] == unit_cols[None, :]).astype(jnp.float32)
    gathered = lax.all_gather(post, "row", axis=1, tiled=True)
    total_cols = super_count * col_width + rhs_width
    solution = jnp.zeros((super_count, row_width, total_cols), jnp.float32)
    for current_sup in range(super_count - 1, -1, -1):
        later_cols = (current_sup + 1) * col_width
        if current_sup == super_count - 1:
            summed = jnp.zeros((full_width, rhs_width), jnp.float32)
        else:
            picks = []
            chosen_rows = []
            for slot_index in range(LEVELS - 1):
                target = ancestor_hops[slot_index][current_sup]
                is_valid = (target < super_count).astype(jnp.float32)
                clamped = jnp.minimum(target, super_count - 1)
                picks.append(
                    lax.dynamic_index_in_dim(
                        masked[:, :, current_sup, :], clamped, 0, keepdims=False
                    )
                    * is_valid
                )
                chosen_rows.append(
                    lax.dynamic_index_in_dim(solution, clamped, 0, keepdims=False)[:, later_cols:]
                )
            blocks = jnp.stack(picks)
            selected = jnp.stack(chosen_rows)
            partial_value = contract(selected, lax.all_gather(blocks, "col", axis=2, tiled=True))
            summed = lax.psum(partial_value, "row")
        split_at = summed.shape[1] - rhs_width
        remaining = jnp.concatenate(
            [-summed[:, :split_at], gathered[current_sup] - summed[:, split_at:]], axis=1
        )
        right = jnp.concatenate([unit_block, remaining], axis=1)
        fresh = jnp.dot(
            lower_inv[current_sup].T, right, precision=HIGHEST, preferred_element_type=jnp.float32
        )
        solution = solution.at[current_sup, :, current_sup * col_width :].set(fresh)
    mean_x = solution[:, :, super_count * col_width :]
    unit_part = solution[:, :, : super_count * col_width]
    squares = jnp.sum(unit_part * unit_part, axis=2)
    variance = lax.psum(squares, "col")
    return (mean_x, variance)


def solution(mesh):
    return jax.shard_map(
        body,
        mesh=mesh,
        in_specs=(
            P(None, "row", None, "col"),
            P(None, None, "row"),
            P(None, None, "row"),
            P(),
            P(None, "row", "col"),
        ),
        out_specs=(P(None, "row", "col"), P(None, "row")),
        check_vma=False,
    )
```

profile of v0, /device:TPU:0, one launch (start us, length us, event | category | flops | bytes accessed | tf_op | source)
XLA Modules:
  0.0 1485.7 jit_solution(14807575500122001028)
XLA Ops:
  15.8 15.3 %broadcast_multiply_fusion = f32[6,512,6,256]{3,1,2,0:T(8,128)} fusion(f32[6,512,6,256]{3,1,2,0:T(8,128)} %param.17, f32[6,512,6]{1,2,0:T(8,128)S(1)} %multiply_bitcast_fusion.10), kind=kLoop, calls=%fused_computation.18 | loop fusion | flops 4718592 | bytes 37822464 | tf_op jit(solution)/shard_map/mul | solution.py:36
  31.1 10.7 fusion.93
  53.4 10.7 broadcast_select_fusion
  78.6 92.2 %all-gather.6.cloned.1.call-done = f32[2,512,2048]{2,1,0:T(8,128)} async-done(((f32[2,512,256]{2,1,0:T(8,128)}), f32[2,512,2048]{2,1,0:T(8,128)}) %all-gather.6.cloned.1.call-update) | async-done | bytes 8388624 | tf_op jit(solution)/shard_map/all_gather | solution.py:67
  170.8 11.2 convolution_bitcast_fusion.4
  199.4 33.4 %all-reduce.7.cloned.1.call-done = f32[2048,264]{0,1:T(8,128)} async-done(((f32[2048,264]{0,1:T(8,128)}), f32[2048,264]{0,1:T(8,128)}) %all-reduce.7.cloned.1.call-update) | async-done | bytes 2162704 | tf_op jit(solution)/shard_map/psum | solution.py:68
  235.5 9.8 fusion.73
  251.2 108.7 %all-gather.8.cloned.1.call-done = f32[2,512,2048]{2,1,0:T(8,128)} async-done(((f32[2,512,256]{2,1,0:T(8,128)}), f32[2,512,2048]{2,1,0:T(8,128)}) %all-gather.8.cloned.1.call-update) | async-done | bytes 8388624 | tf_op jit(solution)/shard_map/all_gather | solution.py:67
  359.9 18.0 %convolution_bitcast_fusion.3 = f32[2048,520]{0,1:T(8,128)} fusion(f32[2,512,2048]{2,1,0:T(8,128)} %all-gather.8.cloned.1.call-done, f32[1,512,520]{1,2,0:T(8,128)} %slice_bitcast_fusion.38, f32[1,512,520]{1,2,0:T(8,128)} %slice_bitcast_fusion.39), kind=kOutput, calls=%fused_computation.57 | convolution fusion | flops 13086760960 | bytes 14778368 | tf_op jit(solution)/shard_map/tiw,tin->wn/dot_general | solution.py:11
  380.1 82.8 %all-reduce.9.cloned.1.call-done = f32[2048,520]{0,1:T(8,128)} async-done(((f32[2048,520]{0,1:T(8,128)}), f32[2048,520]{0,1:T(8,128)}) %all-reduce.9.cloned.1.call-update) | async-done | bytes 4259856 | tf_op jit(solution)/shard_map/psum | solution.py:68
  466.3 13.2 bitcast_dynamic-update-slice_fusion
  485.7 104.2 %all-gather.10.cloned.1.call-done = f32[2,512,2048]{2,1,0:T(8,128)} async-done(((f32[2,512,256]{2,1,0:T(8,128)}), f32[2,512,2048]{2,1,0:T(8,128)}) %all-gather.10.cloned.1.call-update) | async-done | bytes 8388624 | tf_op jit(solution)/shard_map/all_gather | solution.py:67
  589.9 25.4 %convolution_bitcast_fusion.2 = f32[2048,776]{0,1:T(8,128)} fusion(f32[2,512,2048]{2,1,0:T(8,128)} %all-gather.10.cloned.1.call-done, f32[1,512,776]{1,2,0:T(8,128)} %slice_bitcast_fusion.28, f32[1,512,776]{1,2,0:T(8,128)} %slice_bitcast_fusion.29), kind=kOutput, calls=%fused_computation.56 | convolution fusion | flops 19529474048 | bytes 17924096 | tf_op jit(solution)/shard_map/tiw,tin->wn/dot_general | solution.py:11
  623.3 111.1 %all-reduce.11.cloned.1.call-done = f32[2048,776]{0,1:T(8,128)} async-done(((f32[2048,776]{0,1:T(8,128)}), f32[2048,776]{0,1:T(8,128)}) %all-reduce.11.cloned.1.call-update) | async-done | bytes 6357008 | tf_op jit(solution)/shard_map/psum | solution.py:68
  738.6 17.0 %fusion.53 = f32[6,512,1544]{1,2,0:T(8,128)} fusion(f32[6,512,1544]{1,2,0:T(8,128)} %bitcast_dynamic-update-slice_fusion, f32[2048,8]{0,1:T(8,128)S(1)} %slice_subtract_fusion.2, f32[2048,768]{0,1:T(8,128)S(1)} %slice_negate_fusion.2, f32[2048,256]{0,1:T(8,128)S(1)} %fusion.67, f32[6,2048,512]{2,1,0:T(8,128)} %copy-done), kind=kOutput, calls=%fused_computation.63 | convolution fusion | flops 12989792256 | bytes 14761984 | tf_op jit(solution)/shard_map/dot_general | solution.py:74
  762.1 99.4 %all-gather.12.cloned.1.call-done = f32[2,512,2048]{2,1,0:T(8,128)} async-done(((f32[2,512,256]{2,1,0:T(8,128)}), f32[2,512,2048]{2,1,0:T(8,128)}) %all-gather.12.cloned.1.call-update) | async-done | bytes 8388624 | tf_op jit(solution)/shard_map/all_gather | solution.py:67
  861.5 31.5 %convolution_bitcast_fusion.1 = f32[2048,1032]{0,1:T(8,128)} fusion(f32[2,512,2048]{2,1,0:T(8,128)} %all-gather.12.cloned.1.call-done, f32[1,512,1032]{1,2,0:T(8,128)} %slice_bitcast_fusion.26, f32[1,512,1032]{1,2,0:T(8,128)} %slice_bitcast_fusion.27), kind=kOutput, calls=%fused_computation.20 | convolution fusion | flops 25972187136 | bytes 21069824 | tf_op jit(solution)/shard_map/tiw,tin->wn/dot_general | solution.py:11
  894.4 150.9 %all-reduce.13.cloned.1.call-done = f32[2048,1032]{0,1:T(8,128)} async-done(((f32[2048,1032]{0,1:T(8,128)}), f32[2048,1032]{0,1:T(8,128)}) %all-reduce.13.cloned.1.call-update) | async-done | bytes 8454160 | tf_op jit(solution)/shard_map/psum | solution.py:68
  1050.4 20.4 %fusion.41 = f32[6,512,1544]{1,2,0:T(8,128)} fusion(f32[6,512,1544]{1,2,0:T(8,128)} %fusion.53, f32[2048,8]{0,1:T(8,128)S(1)} %slice_subtract_fusion.1, f32[2048,1024]{0,1:T(8,128)S(1)} %slice_negate_fusion.1, f32[2048,256]{0,1:T(8,128)S(1)} %fusion.67, f32[6,2048,512]{2,1,0:T(8,128)} %copy-done), kind=kOutput, calls=%fused_computation.59 | convolution fusion | flops 16212066304 | bytes 17383424 | tf_op jit(solution)/shard_map/dot_general | solution.py:74
  1077.9 94.5 %all-gather.14.cloned.1.call-done = f32[2,512,2048]{2,1,0:T(8,128)} async-done(((f32[2,512,256]{2,1,0:T(8,128)}), f32[2,512,2048]{2,1,0:T(8,128)}) %all-gather.14.cloned.1.call-update) | async-done | bytes 8388624 | tf_op jit(solution)/shard_map/all_gather | solution.py:67
  1172.5 42.1 %convolution_bitcast_fusion = f32[2048,1288]{0,1:T(8,128)} fusion(f32[2,512,2048]{2,1,0:T(8,128)} %all-gather.14.cloned.1.call-done, f32[1,512,1288]{1,2,0:T(8,128)} %slice_bitcast_fusion.24, f32[1,512,1288]{1,2,0:T(8,128)} %slice_bitcast_fusion.25), kind=kOutput, calls=%fused_computation.19 | convolution fusion | flops 32414900224 | bytes 24215552 | tf_op jit(solution)/shard_map/tiw,tin->wn/dot_general | solution.py:11
  1214.6 186.2 %all-reduce.15.cloned.1.call-done = f32[2048,1288]{0,1:T(8,128)} async-done(((f32[2048,1288]{0,1:T(8,128)}), f32[2048,1288]{0,1:T(8,128)}) %all-reduce.15.cloned.1.call-update) | async-done | bytes 10551312 | tf_op jit(solution)/shard_map/psum | solution.py:68
  1406.7 23.9 %fusion.47 = f32[6,512,1544]{1,2,0:T(8,128)} fusion(f32[6,512,1544]{1,2,0:T(8,128)} %fusion.41, f32[2048,8]{0,1:T(8,128)S(1)} %slice_subtract_fusion, f32[2048,1280]{0,1:T(8,128)S(1)} %slice_negate_fusion, f32[2048,256]{0,1:T(8,128)S(1)} %fusion.67, f32[6,2048,512]{2,1,0:T(8,128)} %copy-done), kind=kOutput, calls=%fused_computation.61 | convolution fusion | flops 19434340352 | bytes 20004864 | tf_op jit(solution)/shard_map/dot_general | solution.py:74
  1440.9 37.7 %psum.47 = f32[6,512]{1,0:T(8,128)} all-reduce(f32[6,512]{1,0:T(8,128)S(1)} %fusion), channel_id=1, replica_groups=mesh['row'=4,'col'=8] {'col'}, use_global_device_ids=true, to_apply=%region_10.11 | all-reduce | flops 3072 | bytes 24576 | tf_op jit(solution)/shard_map/psum | solution.py:81
  (85 shorter events, 108.3 us)
Async XLA Ops:
  7.2 163.6 %all-gather.6.cloned.1.call-start = ((), (), s32[]{:S(2)}) async-start(), calls=%async_computation | async-start | bytes 9437184 | tf_op jit(solution)/shard_map/all_gather | solution.py:67
  41.8 1.3 copy-start.4
  43.0 189.8 %all-reduce.7.cloned.1.call-start = ((), (), s32[]{:S(2)}) async-start(), calls=%async_computation.1 | async-start | bytes 4325376 | tf_op jit(solution)/shard_map/psum | solution.py:68
  51.6 0.8 copy-start.2
  64.1 8.5 copy-start
  182.0 177.9 %all-gather.8.cloned.1.call-start = ((), (), s32[]{:S(2)}) async-start(), calls=%async_computation.2 | async-start | bytes 9437184 | tf_op jit(solution)/shard_map/all_gather | solution.py:67
  190.4 42.4 %copy-start.3 = (f32[6,2048,8]{1,2,0:T(8,128)S(1)}, f32[6,2048,8]{1,2,0:T(8,128)}, u32[]{:S(2)}) copy-start(f32[6,2048,8]{1,2,0:T(8,128)} %copy-done.2) | copy-start | bytes 1179652
  190.4 272.5 %all-reduce.9.cloned.1.call-start = ((), (), s32[]{:S(2)}) async-start(), calls=%async_computation.3 | async-start | bytes 8519680 | tf_op jit(solution)/shard_map/psum | solution.py:68
  378.0 1.0 copy-start.1
  378.0 211.9 %all-gather.10.cloned.1.call-start = ((), (), s32[]{:S(2)}) async-start(), calls=%async_computation.4 | async-start | bytes 9437184 | tf_op jit(solution)/shard_map/all_gather | solution.py:67
  380.0 354.3 %all-reduce.11.cloned.1.call-start = ((), (), s32[]{:S(2)}) async-start(), calls=%async_computation.5 | async-start | bytes 12713984 | tf_op jit(solution)/shard_map/psum | solution.py:68
  615.3 246.2 %all-gather.12.cloned.1.call-start = ((), (), s32[]{:S(2)}) async-start(), calls=%async_computation.6 | async-start | bytes 9437184 | tf_op jit(solution)/shard_map/all_gather | solution.py:67
  623.2 422.1 %all-reduce.13.cloned.1.call-start = ((), (), s32[]{:S(2)}) async-start(), calls=%async_computation.7 | async-start | bytes 16908288 | tf_op jit(solution)/shard_map/psum | solution.py:68
  893.0 279.4 %all-gather.14.cloned.1.call-start = ((), (), s32[]{:S(2)}) async-start(), calls=%async_computation.8 | async-start | bytes 9437184 | tf_op jit(solution)/shard_map/all_gather | solution.py:67
  894.2 506.6 %all-reduce.15.cloned.1.call-start = ((), (), s32[]{:S(2)}) async-start(), calls=%async_computation.9 | async-start | bytes 21102592 | tf_op jit(solution)/shard_map/psum | solution.py:68
Sparse Core Ops, SparseCore 0:
  43.1 127.6 all-gather.5
  182.1 50.6 all-reduce.6
  234.9 124.9 all-gather.7
  378.1 84.7 all-reduce.8
  464.8 125.0 all-gather.9
  615.5 118.8 all-reduce.10
  736.4 125.1 all-gather.11
  893.2 152.0 all-reduce.12
  1047.4 125.0 all-gather.13
  1214.7 185.9 all-reduce.14
where the time goes:
time: 1490 us
  waiting for transfers between devices  1060 us (71%)
  matrix products  216 us (14%)
  other arithmetic  70.2 us (5%)
  local copies, waits for them, and re-layouts  61.6 us (4%)
  blocking collectives  46.2 us (3%)
  between operations  27.1 us (2%)
    psum x5, waiting for transfers between devices, body(): summed = lax.psum(partial_value, 'row')  564 us
    all_gather x5, waiting for transfers between devices, body(): lax.all_gather(blocks, 'col', axis=2, tiled=True)  499 us
    dot_general x5, matrix products, contract(): return jnp.einsum('tiw,tin->wn', panel_piece, selected, precision=HIGHEST)  128 us
    dot_general x6, matrix products, body(): jnp.dot(lower_inv[current_sup].T, right, precision=HIGHEST, preferred_ele...  88.2 us
    psum x1, blocking collectives, body(): variance = lax.psum(squares, 'col')  37.7 us
  transfers between devices with their start and end apart: 10, of which 10 were waited for; matrix products, arithmetic and copies ran while one was open for 9% of the time, Pallas kernels for 0%

commit v1 on v0

--- a/solution.py
+++ b/solution.py
@@ -64,7 +64,9 @@
                 )
             blocks = jnp.stack(picks)
             selected = jnp.stack(chosen_rows)
-            partial_value = contract(selected, lax.all_gather(blocks, "col", axis=2, tiled=True))
+            partial_value = contract(
+                selected, jnp.concatenate(lax.all_gather(blocks, "col"), axis=2)
+            )
             summed = lax.psum(partial_value, "row")
         split_at = summed.shape[1] - rhs_width
         remaining = jnp.concatenate(

time: 1490 us -> 1440 us (0.966)
  waiting for transfers between devices: 1060 us -> 925 us
  local copies, waits for them, and re-layouts: 61.6 us -> 156 us
    all_gather x5, waiting for transfers between devices: 499 us -> 405 us  [body(): lax.all_gather(blocks, 'col')]
    all_gather x0 -> x5, local copies, waits for them, and re-layouts: none -> 57.9 us  [body(): lax.all_gather(blocks, 'col')]
    reshape x0 -> x5, local copies, waits for them, and re-layouts: none -> 46.7 us  [body(): jnp.concatenate(lax.all_gather(blocks, 'col'), axis=2)]
    psum x5, waiting for transfers between devices: 564 us -> 520 us  [body(): summed = lax.psum(partial_value, 'row')]
  transfers between devices with their start and end apart: 10 -> 10, of which waited for: 10 -> 10; matrix products, arithmetic and copies ran while one was open for 9% -> 20% of each run, Pallas kernels for 0% -> 0%
where the time goes in v1:
time: 1440 us; the launch traced here: 1430 us
  waiting for transfers between devices  925 us (64%)
  matrix products  204 us (14%)
  local copies, waits for them, and re-layouts  156 us (11%)
  other arithmetic  72.9 us (5%)
  blocking collectives  45.6 us (3%)
  between operations  27.4 us (2%)
    psum x5, waiting for transfers between devices, body(): summed = lax.psum(partial_value, 'row')  520 us
    all_gather x5, waiting for transfers between devices, body(): lax.all_gather(blocks, 'col')  405 us
    dot_general x5, matrix products, contract(): return jnp.einsum('tiw,tin->wn', panel_piece, selected, precision=HIGHEST)  116 us
    dot_general x6, matrix products, body(): jnp.dot(lower_inv[current_sup].T, right, precision=HIGHEST, preferred_ele...  88 us
    all_gather x5, local copies, waits for them, and re-layouts, body(): lax.all_gather(blocks, 'col')  57.9 us
    reshape x5, local copies, waits for them, and re-layouts, body(): jnp.concatenate(lax.all_gather(blocks, 'col'), axis=2)  46.7 us
    psum x1, blocking collectives, body(): variance = lax.psum(squares, 'col')  37.7 us
  transfers between devices with their start and end apart: 10, of which 10 were waited for; matrix products, arithmetic and copies ran while one was open for 20% of the time, Pallas kernels for 0%

profile of v1, /device:TPU:0, one launch (start us, length us, event | category | flops | bytes accessed | tf_op | source)
XLA Modules:
  0.0 1431.6 jit_solution(7561066047648841683)
XLA Ops:
  15.8 15.3 %broadcast_multiply_fusion = f32[6,512,6,256]{3,1,2,0:T(8,128)} fusion(f32[6,512,6,256]{3,1,2,0:T(8,128)} %param.17, f32[6,512,6]{1,2,0:T(8,128)S(1)} %multiply_bitcast_fusion.10), kind=kLoop, calls=%fused_computation.18 | loop fusion | flops 4718592 | bytes 37822464 | tf_op jit(solution)/shard_map/mul | solution.py:36
  88.0 83.6 %all-gather.11.cloned.1.call-done = f32[16,512,256]{2,1,0:T(8,128)} async-done(((f32[2,512,256]{2,1,0:T(8,128)}), f32[16,512,256]{2,1,0:T(8,128)}) %all-gather.11.cloned.1.call-update) | async-done | bytes 8388624 | tf_op jit(solution)/shard_map/all_gather | solution.py:68
  215.1 81.3 %all-gather.13.cloned.1.call-done = f32[16,512,256]{2,1,0:T(8,128)} async-done(((f32[2,512,256]{2,1,0:T(8,128)}), f32[16,512,256]{2,1,0:T(8,128)}) %all-gather.13.cloned.1.call-update) | async-done | bytes 8388624 | tf_op jit(solution)/shard_map/all_gather | solution.py:68
  296.4 11.6 copy.33
  317.5 31.9 %all-reduce.7.cloned.1.call-done = f32[2048,264]{0,1:T(8,128)} async-done(((f32[2048,264]{0,1:T(8,128)}), f32[2048,264]{0,1:T(8,128)}) %all-reduce.7.cloned.1.call-update) | async-done | bytes 2162704 | tf_op jit(solution)/shard_map/psum | solution.py:70
  365.9 15.4 %convolution_bitcast_fusion.3 = f32[2048,520]{0,1:T(8,128)} fusion(f32[2,512,2048]{2,1,0:T(8,128)S(1)} %bitcast.220, f32[1,512,520]{1,2,0:T(8,128)S(1)} %slice_bitcast_fusion.38, f32[1,512,520]{1,2,0:T(8,128)S(1)} %slice_bitcast_fusion.39), kind=kOutput, calls=%fused_computation.62 | convolution fusion | flops 13086760960 | bytes 14778368 | tf_op jit(solution)/shard_map/tiw,tin->wn/dot_general | solution.py:11
  389.5 86.5 %all-gather.15.cloned.1.call-done = f32[16,512,256]{2,1,0:T(8,128)} async-done(((f32[2,512,256]{2,1,0:T(8,128)}), f32[16,512,256]{2,1,0:T(8,128)}) %all-gather.15.cloned.1.call-update) | async-done | bytes 8388624 | tf_op jit(solution)/shard_map/all_gather | solution.py:68
  476.0 11.6 copy.32
  496.9 66.1 %all-reduce.9.cloned.1.call-done = f32[2048,520]{0,1:T(8,128)} async-done(((f32[2048,520]{0,1:T(8,128)}), f32[2048,520]{0,1:T(8,128)}) %all-reduce.9.cloned.1.call-update) | async-done | bytes 4259856 | tf_op jit(solution)/shard_map/psum | solution.py:70
  566.4 13.0 bitcast_dynamic-update-slice_fusion
  583.5 22.7 %convolution_bitcast_fusion.2 = f32[2048,776]{0,1:T(8,128)} fusion(f32[2,512,2048]{2,1,0:T(8,128)S(1)} %bitcast.222, f32[1,512,776]{1,2,0:T(8,128)S(1)} %slice_bitcast_fusion.28, f32[1,512,776]{1,2,0:T(8,128)S(1)} %slice_bitcast_fusion.29), kind=kOutput, calls=%fused_computation.61 | convolution fusion | flops 19529474048 | bytes 17924096 | tf_op jit(solution)/shard_map/tiw,tin->wn/dot_general | solution.py:11
  607.6 82.0 %all-gather.17.cloned.1.call-done = f32[16,512,256]{2,1,0:T(8,128)} async-done(((f32[2,512,256]{2,1,0:T(8,128)}), f32[16,512,256]{2,1,0:T(8,128)}) %all-gather.17.cloned.1.call-update) | async-done | bytes 8388624 | tf_op jit(solution)/shard_map/all_gather | solution.py:68
  689.6 11.6 copy.31
  710.6 100.3 %all-reduce.11.cloned.1.call-done = f32[2048,776]{0,1:T(8,128)} async-done(((f32[2048,776]{0,1:T(8,128)}), f32[2048,776]{0,1:T(8,128)}) %all-reduce.11.cloned.1.call-update) | async-done | bytes 6357008 | tf_op jit(solution)/shard_map/psum | solution.py:70
  815.3 16.9 %fusion.53 = f32[6,512,1544]{1,2,0:T(8,128)} fusion(f32[6,512,1544]{1,2,0:T(8,128)} %bitcast_dynamic-update-slice_fusion, f32[2048,8]{0,1:T(8,128)S(1)} %slice_subtract_fusion.2, f32[2048,768]{0,1:T(8,128)S(1)} %slice_negate_fusion.2, f32[2048,256]{0,1:T(8,128)S(1)} %fusion.67, f32[6,2048,512]{2,1,0:T(8,128)} %copy-done), kind=kOutput, calls=%fused_computation.68 | convolution fusion | flops 12989792256 | bytes 14761984 | tf_op jit(solution)/shard_map/dot_general | solution.py:76
  836.3 30.2 %convolution_bitcast_fusion.1 = f32[2048,1032]{0,1:T(8,128)} fusion(f32[2,512,2048]{2,1,0:T(8,128)S(1)} %bitcast.224, f32[1,512,1032]{1,2,0:T(8,128)S(1)} %slice_bitcast_fusion.26, f32[1,512,1032]{1,2,0:T(8,128)S(1)} %slice_bitcast_fusion.27), kind=kOutput, calls=%fused_computation.20 | convolution fusion | flops 25972187136 | bytes 21069824 | tf_op jit(solution)/shard_map/tiw,tin->wn/dot_general | solution.py:11
  866.5 71.2 %all-gather.19.cloned.1.call-done = f32[16,512,256]{2,1,0:T(8,128)} async-done(((f32[2,512,256]{2,1,0:T(8,128)}), f32[16,512,256]{2,1,0:T(8,128)}) %all-gather.19.cloned.1.call-update) | async-done | bytes 8388624 | tf_op jit(solution)/shard_map/all_gather | solution.py:68
  937.7 11.6 copy.30
  958.5 133.8 %all-reduce.13.cloned.1.call-done = f32[2048,1032]{0,1:T(8,128)} async-done(((f32[2048,1032]{0,1:T(8,128)}), f32[2048,1032]{0,1:T(8,128)}) %all-reduce.13.cloned.1.call-update) | async-done | bytes 8454160 | tf_op jit(solution)/shard_map/psum | solution.py:70
  1097.6 20.5 %fusion.41 = f32[6,512,1544]{1,2,0:T(8,128)} fusion(f32[6,512,1544]{1,2,0:T(8,128)} %fusion.53, f32[2048,8]{0,1:T(8,128)S(1)} %slice_subtract_fusion.1, f32[2048,1024]{0,1:T(8,128)S(1)} %slice_negate_fusion.1, f32[2048,256]{0,1:T(8,128)S(1)} %fusion.67, f32[6,2048,512]{2,1,0:T(8,128)} %copy-done), kind=kOutput, calls=%fused_computation.64 | convolution fusion | flops 16212066304 | bytes 17383424 | tf_op jit(solution)/shard_map/dot_general | solution.py:76
  1122.2 36.4 %convolution_bitcast_fusion = f32[2048,1288]{0,1:T(8,128)} fusion(f32[2,512,2048]{2,1,0:T(8,128)S(1)} %bitcast.226, f32[1,512,1288]{1,2,0:T(8,128)S(1)} %slice_bitcast_fusion.24, f32[1,512,1288]{1,2,0:T(8,128)S(1)} %slice_bitcast_fusion.25), kind=kOutput, calls=%fused_computation.19 | convolution fusion | flops 32414900224 | bytes 24215552 | tf_op jit(solution)/shard_map/tiw,tin->wn/dot_general | solution.py:11
  1158.6 188.1 %all-reduce.15.cloned.1.call-done = f32[2048,1288]{0,1:T(8,128)} async-done(((f32[2048,1288]{0,1:T(8,128)}), f32[2048,1288]{0,1:T(8,128)}) %all-reduce.15.cloned.1.call-update) | async-done | bytes 10551312 | tf_op jit(solution)/shard_map/psum | solution.py:70
  1352.7 23.9 %fusion.47 = f32[6,512,1544]{1,2,0:T(8,128)} fusion(f32[6,512,1544]{1,2,0:T(8,128)} %fusion.41, f32[2048,8]{0,1:T(8,128)S(1)} %slice_subtract_fusion, f32[2048,1280]{0,1:T(8,128)S(1)} %slice_negate_fusion, f32[2048,256]{0,1:T(8,128)S(1)} %fusion.67, f32[6,2048,512]{2,1,0:T(8,128)} %copy-done), kind=kOutput, calls=%fused_computation.66 | convolution fusion | flops 19434340352 | bytes 20004864 | tf_op jit(solution)/shard_map/dot_general | solution.py:76
  1386.9 37.7 %psum.47 = f32[6,512]{1,0:T(8,128)} all-reduce(f32[6,512]{1,0:T(8,128)S(1)} %fusion), channel_id=1, replica_groups=mesh['row'=4,'col'=8] {'col'}, use_global_device_ids=true, to_apply=%region_10.11 | all-reduce | flops 3072 | bytes 24576 | tf_op jit(solution)/shard_map/psum | solution.py:83
  (113 shorter events, 201.2 us)
Async XLA Ops:
  7.2 164.4 %all-gather.11.cloned.1.call-start = ((), (), s32[]{:S(2)}) async-start(), calls=%async_computation.5 | async-start | bytes 9437184 | tf_op jit(solution)/shard_map/all_gather | solution.py:68
  44.2 8.7 copy-start.3
  44.2 252.2 %all-gather.13.cloned.1.call-start = ((), (), s32[]{:S(2)}) async-start(), calls=%async_computation.6 | async-start | bytes 9437184 | tf_op jit(solution)/shard_map/all_gather | solution.py:68
  52.8 296.6 %all-reduce.7.cloned.1.call-start = ((), (), s32[]{:S(2)}) async-start(), calls=%async_computation | async-start | bytes 4325376 | tf_op jit(solution)/shard_map/psum | solution.py:70
  60.9 0.8 copy-start.1
  73.5 8.4 copy-start
  203.8 272.2 %all-gather.15.cloned.1.call-start = ((), (), s32[]{:S(2)}) async-start(), calls=%async_computation.7 | async-start | bytes 9437184 | tf_op jit(solution)/shard_map/all_gather | solution.py:68
  206.2 356.8 %all-reduce.9.cloned.1.call-start = ((), (), s32[]{:S(2)}) async-start(), calls=%async_computation.1 | async-start | bytes 8519680 | tf_op jit(solution)/shard_map/psum | solution.py:70
  308.0 41.4 %copy-start.2 = (f32[6,2048,8]{1,2,0:T(8,128)S(1)}, f32[6,2048,8]{1,2,0:T(8,128)}, u32[]{:S(2)}) copy-start(f32[6,2048,8]{1,2,0:T(8,128)} %copy-done.1) | copy-start | bytes 1179652
  352.1 13.6 slice-start
  361.9 4.0 slice-start.1
  381.4 308.3 %all-gather.17.cloned.1.call-start = ((), (), s32[]{:S(2)}) async-start(), calls=%async_computation.8 | async-start | bytes 9437184 | tf_op jit(solution)/shard_map/all_gather | solution.py:68
  389.0 421.8 %all-reduce.11.cloned.1.call-start = ((), (), s32[]{:S(2)}) async-start(), calls=%async_computation.2 | async-start | bytes 12713984 | tf_op jit(solution)/shard_map/psum | solution.py:70
  566.4 17.0 %slice-start.2 = ((s8[8388608]{0:T(1024)(128)(4,1)}), s8[4194304]{0:T(1024)(128)(4,1)S(1)}, s32[]{:S(2)}) async-start(s8[8388608]{0:T(1024)(128)(4,1)} %bitcast.221), calls=%async_computation.12 | async-start | bytes 8388608
  579.4 4.1 slice-start.3
  606.2 331.5 %all-gather.19.cloned.1.call-start = ((), (), s32[]{:S(2)}) async-start(), calls=%async_computation.9 | async-start | bytes 9437184 | tf_op jit(solution)/shard_map/all_gather | solution.py:68
  607.3 485.0 %all-reduce.13.cloned.1.call-start = ((), (), s32[]{:S(2)}) async-start(), calls=%async_computation.3 | async-start | bytes 16908288 | tf_op jit(solution)/shard_map/psum | solution.py:70
  811.7 24.5 %slice-start.4 = ((s8[8388608]{0:T(1024)(128)(4,1)}), s8[4194304]{0:T(1024)(128)(4,1)S(1)}, s32[]{:S(2)}) async-start(s8[8388608]{0:T(1024)(128)(4,1)} %bitcast.223), calls=%async_computation.14 | async-start | bytes 8388608
  815.3 20.9 %slice-start.5 = ((s8[8388608]{0:T(1024)(128)(4,1)}), s8[4194304]{0:T(1024)(128)(4,1)S(1)}, s32[]{:S(2)}) async-start(s8[8388608]{0:T(1024)(128)(4,1)} %bitcast.223), calls=%async_computation.15 | async-start | bytes 8388608
  866.4 480.3 %all-reduce.15.cloned.1.call-start = ((), (), s32[]{:S(2)}) async-start(), calls=%async_computation.4 | async-start | bytes 21102592 | tf_op jit(solution)/shard_map/psum | solution.py:70
  1093.2 29.0 %slice-start.6 = ((s8[8388608]{0:T(1024)(128)(4,1)}), s8[4194304]{0:T(1024)(128)(4,1)S(1)}, s32[]{:S(2)}) async-start(s8[8388608]{0:T(1024)(128)(4,1)} %bitcast.225), calls=%async_computation.16 | async-start | bytes 8388608
  1097.6 24.6 %slice-start.7 = ((s8[8388608]{0:T(1024)(128)(4,1)}), s8[4194304]{0:T(1024)(128)(4,1)S(1)}, s32[]{:S(2)}) async-start(s8[8388608]{0:T(1024)(128)(4,1)} %bitcast.225), calls=%async_computation.17 | async-start | bytes 8388608
Sparse Core Ops, SparseCore 0:
  44.4 127.1 all-gather.10
  173.7 122.6 all-gather.12
  298.8 50.6 all-reduce.6
  351.4 124.5 all-gather.14
  478.2 84.7 all-reduce.8
  565.0 124.5 all-gather.16
  692.0 118.8 all-reduce.10
  813.0 124.6 all-gather.18
  940.2 152.0 all-reduce.12
  1158.7 187.9 all-reduce.14
